TPU v7x, 32 devices: a whole 2x2x4 slice. The times are simulated.
32 devices in a mesh: row: 8 (over z, y), col: 4 (over x, core).
Axes of the slice: x: 2, y: 2, z: 4, core: 2. Of those that a mesh axis runs over, the one named last changes fastest.
Arguments:
- upper: bfloat16 [4096, 8, 4, 128], P('row', None, 'col'), as said below
- signs: int32 [4096, 512], P(('row', 'col')), may hold values from 0 to 1
- weights: float32 [4096], P(('row', 'col')), may hold values from 0.5 to 2
- components: float32 [2], replicated, may hold values from 0.3 to 3
Outputs:
- applied: float32 [4096, 512], P(('row', 'col'))
Inputs may be any that keep to these rules, and one draw needn't show every extreme that they name: upper's first dimension and its flattened column index count the same samples in the same order.
All inputs are finite; a program needn't handle non-finite values.
Results may differ from a plain program's by a relative error of at most 0.0055.
Values may be sent and summed in bfloat16 or wider, within the bound.
No kernel may reach another device: no remote copies, remote signals or barrier semaphores. Data moves between devices by JAX's collectives and lax.ppermute only.
A program may use at most 128 MiB of HBM per device.

v0:
```python
import jax
import jax.numpy as jnp
from jax import lax
from jax.sharding import PartitionSpec as P


def body(upper, signs, weights, components):
    rows, ntiles, single, fine = upper.shape
    row_index = lax.axis_index("row")
    col_index = lax.axis_index("col")
    flat = upper.reshape(rows, ntiles * fine)
    probes = ((2 * signs - 1).astype(jnp.float32) * weights[:, None]).astype(jnp.bfloat16)
    q_rows = lax.all_gather(probes, "col", axis=0, tiled=True)
    zero = jnp.zeros((), jnp.bfloat16)
    rowpos = lax.broadcasted_iota(jnp.int32, (rows, ntiles, fine), 0)
    tilepos = lax.broadcasted_iota(jnp.int32, (rows, ntiles, fine), 1)
    colpos = col_index * fine + lax.broadcasted_iota(jnp.int32, (rows, ntiles, fine), 2)
    beyond = tilepos > row_index
    onside = tilepos == row_index
    keep_up = (beyond | onside & (colpos >= rowpos)).reshape(rows, ntiles * fine)
    keep_strict = (beyond | onside & (colpos > rowpos)).reshape(rows, ntiles * fine)
    masked_a = jnp.where(keep_up, flat, zero)
    masked_b = jnp.where(keep_strict, flat, zero)
    columns = masked_a
    direct = jnp.dot(
        columns,
        lax.all_gather(probes, "row", axis=0, tiled=True),
        preferred_element_type=jnp.float32,
    )
    columns = masked_b
    mirrored = lax.psum_scatter(
        lax.dot_general(
            columns, q_rows, (((0,), (0,)), ((), ())), preferred_element_type=jnp.float32
        ).astype(jnp.bfloat16),
        "row",
        scatter_dimension=0,
        tiled=True,
    ).astype(jnp.float32)
    summed = lax.psum_scatter(direct, "col", scatter_dimension=0, tiled=True)
    return components[0] * (summed + mirrored) + components[1] * probes.astype(jnp.float32)


def solution(mesh):
    return jax.shard_map(
        body,
        mesh=mesh,
        in_specs=(P("row", None, "col", None), P(("row", "col"), None), P(("row", "col")), P()),
        out_specs=P(("row", "col"), None),
        check_vma=False,
    )
```

profile of v0, /device:TPU:0, one launch (start us, length us, event | category | flops | bytes accessed | tf_op | source)
XLA Modules:
  0.0 154.1 jit_solution(2603484826157275666)
XLA Ops:
  6.5 0.0 copy-start.3
  6.5 0.0 all-gather.2.cloned.1.call-start
  6.5 1.8 %multiply_convert_fusion = bf16[128,512]{1,0:T(8,128)(2,1)} fusion(s32[128,512]{1,0:T(8,128)} %param.5, f32[128]{0:T(128)} %param.6), kind=kLoop, calls=%fused_computation.23 | loop fusion | flops 327680 | bytes 393728 | tf_op jit(solution)/shard_map/convert_element_type | solution.py:12
  8.3 0.0 all-gather.2.cloned.1.call-update
  8.3 0.0 reduce-scatter.5.cloned.1.call-start
  8.4 8.8 %all_gather.7 = bf16[512,512]{1,0:T(8,128)(2,1)S(1)} all-gather(bf16[128,512]{1,0:T(8,128)(2,1)} %multiply_convert_fusion), channel_id=1, replica_groups=mesh['row'=8,'col'=4] {'col'}, dimensions={0}, use_global_device_ids=true | all-gather | bytes 655360 | tf_op jit(solution)/shard_map/all_gather | solution.py:13
  17.3 0.1 broadcast_bitcast_fusion.1
  17.3 0.1 broadcast_bitcast_fusion.2
  17.4 0.0 copy-done.3
  17.4 1.8 %convolution_convert_fusion = bf16[1024,512]{1,0:T(8,128)(2,1)} fusion(bf16[512,512]{1,0:T(8,128)(2,1)S(1)} %all_gather.7, s32[1024]{0:T(1024)S(1)} %broadcast_bitcast_fusion, pred[1024]{0:T(1024)(128)(4,1)S(1)} %broadcast_bitcast_fusion.1, pred[1024]{0:T(1024)(128)(4,1)S(1)} %broadcast_bitcast_fusion.2, bf16[64,8,8,128]{3,2,1,0:T(8,128)(2,1)S(1)} %bitcast.22), kind=kOutput, calls=%fused_computation.8 | convolution fusion | flops 539492352 | bytes 2627584 | tf_op jit(solution)/shard_map/dot_general | solution.py:32
  19.2 0.0 reduce-scatter.5.cloned.1.call-update
  19.2 0.0 reduce-scatter.3.cloned.1.call-start
  19.3 33.1 %all-gather.2.cloned.1.call-done = bf16[1024,512]{1,0:T(8,128)(2,1)} async-done(((bf16[128,512]{1,0:T(8,128)(2,1)}), bf16[1024,512]{1,0:T(8,128)(2,1)}) %all-gather.2.cloned.1.call-update) | async-done | bytes 1048592 | tf_op jit(solution)/shard_map/all_gather | solution.py:27
  52.4 3.0 %fusion.7 = f32[512,512]{1,0:T(8,128)} fusion(bf16[1024,512]{1,0:T(8,128)(2,1)} %all-gather.2.cloned.1.call-done, s32[1024]{0:T(1024)S(1)} %broadcast_bitcast_fusion, pred[1024]{0:T(1024)(128)(4,1)S(1)} %broadcast_bitcast_fusion.1, pred[1024]{0:T(1024)(128)(4,1)S(1)} %broadcast_bitcast_fusion.2, bf16[64,8,8,128]{3,2,1,0:T(8,128)(2,1)S(1)} %bitcast.23), kind=kOutput, calls=%fused_computation.9 | convolution fusion | flops 538968064 | bytes 3151872 | tf_op jit(solution)/shard_map/dot_general | solution.py:25
  55.3 0.0 copy-start.2
  55.3 0.0 copy-start
  55.3 0.0 reduce-scatter.3.cloned.1.call-update
  55.4 0.6 copy-done.2
  56.0 0.6 fusion.23
  56.6 61.3 %reduce-scatter.5.cloned.1.call-done = bf16[128,512]{1,0:T(8,128)(2,1)} async-done(((bf16[1024,512]{1,0:T(8,128)(2,1)}), bf16[128,512]{1,0:T(8,128)(2,1)}) %reduce-scatter.5.cloned.1.call-update) | async-done | bytes 131088 | tf_op jit(solution)/shard_map/reduce_scatter | solution.py:31
  117.9 26.6 %reduce-scatter.3.cloned.1.call-done = f32[128,512]{1,0:T(8,128)} async-done(((f32[512,512]{1,0:T(8,128)}), f32[128,512]{1,0:T(8,128)}) %reduce-scatter.3.cloned.1.call-update) | async-done | bytes 262160 | tf_op jit(solution)/shard_map/reduce_scatter | solution.py:39
  144.5 0.0 copy-done
  144.5 0.0 copy-done.1
  144.5 3.1 %multiply_add_fusion = f32[128,512]{1,0:T(8,128)} fusion(f32[128,512]{1,0:T(8,128)} %reduce-scatter.3.cloned.1.call-done, bf16[128,512]{1,0:T(8,128)(2,1)} %reduce-scatter.5.cloned.1.call-done, f32[]{:T(128)} %bitcast.4, f32[]{:T(128)} %bitcast, f32[128]{0:T(128)S(1)} %copy-done.1, s32[128,512]{1,0:T(8,128)S(1)} %copy-done), kind=kLoop, calls=%fused_computation.22 | loop fusion | flops 720896 | bytes 918024 | tf_op jit(solution)/shard_map/add | solution.py:40
  (4 shorter events, 0.0 us)
Async XLA Ops:
  6.5 10.9 %copy-start.3 = (bf16[512,8,1,128]{3,1,2,0:T(8,128)(2,1)S(1)}, bf16[512,8,1,128]{3,1,2,0:T(8,128)(2,1)}, u32[]{:S(2)}) copy-start(bf16[512,8,1,128]{3,1,2,0:T(8,128)(2,1)} %param.4) | copy-start | bytes 3145732
  6.5 45.8 %all-gather.2.cloned.1.call-start = ((), (), s32[]{:S(2)}) async-start(), calls=%async_computation.2 | async-start | bytes 1179648 | tf_op jit(solution)/shard_map/all_gather | solution.py:27
  8.3 109.5 %reduce-scatter.5.cloned.1.call-start = ((), (), s32[]{:S(2)}) async-start(), calls=%async_computation.4 | async-start | bytes 1179648 | tf_op jit(solution)/shard_map/reduce_scatter | solution.py:31
  19.2 125.3 %reduce-scatter.3.cloned.1.call-start = ((), (), s32[]{:S(2)}) async-start(), calls=%async_computation.3 | async-start | bytes 1310720 | tf_op jit(solution)/shard_map/reduce_scatter | solution.py:39
  55.3 0.7 copy-start.2
  55.3 89.2 %copy-start = (s32[128,512]{1,0:T(8,128)S(1)}, s32[128,512]{1,0:T(8,128)}, u32[]{:S(2)}) copy-start(s32[128,512]{1,0:T(8,128)} %param.5) | copy-start | bytes 786436
  55.3 89.2 %copy-start.1 = (f32[128]{0:T(128)S(1)}, f32[128]{0:T(128)}, u32[]{:S(2)}) copy-start(f32[128]{0:T(128)} %param.6) | copy-start | bytes 1540
Sparse Core Ops, SparseCore 0:
  9.5 42.8 all-gather.1
  55.8 62.0 reduce-scatter.4
  120.6 23.8 reduce-scatter.2
where the time goes:
time: 154 us
  waiting for transfers between devices  121 us (79%)
  between operations  13.1 us (9%)
  blocking collectives  8.83 us (6%)
  other arithmetic  4.85 us (3%)
  matrix products  4.75 us (3%)
    reduce_scatter x1, waiting for transfers between devices, body(): lax.psum_scatter(lax.dot_general(columns, q_rows, (((0,), (0,)), ((), ())...  61.3 us
    all_gather x1, waiting for transfers between devices, body(): lax.all_gather(probes, 'row', axis=0, tiled=True)  33.1 us
    reduce_scatter x1, waiting for transfers between devices, body(): summed = lax.psum_scatter(direct, 'col', scatter_dimension=0, tiled=True)  26.6 us
    all_gather x1, blocking collectives, body(): q_rows = lax.all_gather(probes, 'col', axis=0, tiled=True)  8.83 us
  transfers between devices with their start and end apart: 3, of which 3 were waited for; matrix products, arithmetic and copies ran while one was open for 4% of the time, Pallas kernels for 0%

commit v1 on v0

--- a/solution.py
+++ b/solution.py
@@ -2,6 +2,23 @@
 import jax.numpy as jnp
 from jax import lax
 from jax.sharding import PartitionSpec as P
+
+
+def laid_out(blocks, dim):
+    blocks = jnp.moveaxis(blocks, 0, dim)
+    lengths = blocks.shape
+    return blocks.reshape(*lengths[:dim], lengths[dim] * lengths[dim + 1], *lengths[dim + 2 :])
+
+
+def gather_around(x, axis, dim):
+    size = lax.axis_size(axis)
+    right = [(i, (i + 1) % size) for i in range(size)]
+    blocks = [x]
+    while len(blocks) < size:
+        blocks.append(lax.ppermute(blocks[-1], axis, right))
+    index = lax.axis_index(axis)
+    blocks = jnp.stack(blocks)[(index - jnp.arange(size)) % size]
+    return laid_out(blocks, dim)
 
 
 def body(upper, signs, weights, components):
@@ -22,11 +39,7 @@
     masked_a = jnp.where(keep_up, flat, zero)
     masked_b = jnp.where(keep_strict, flat, zero)
     columns = masked_a
-    direct = jnp.dot(
-        columns,
-        lax.all_gather(probes, "row", axis=0, tiled=True),
-        preferred_element_type=jnp.float32,
-    )
+    direct = jnp.dot(columns, gather_around(probes, "row", 0), preferred_element_type=jnp.float32)
     columns = masked_b
     mirrored = lax.psum_scatter(
         lax.dot_general(

time: 154 us -> 123 us (0.80)
  waiting for transfers between devices: 121 us -> 86.8 us
  starting transfers between devices: 0.09 us -> 4.65 us
  blocking collectives: 8.83 us -> 7.16 us
    reduce_scatter x1, waiting for transfers between devices: 61.3 us -> 12.1 us  [body(): lax.psum_scatter(lax.dot_general(columns, q_rows, (((0,), (0,)), ((), ())...]
    ppermute x0 -> x7, waiting for transfers between devices: none -> 48 us  [gather_around(): blocks.append(lax.ppermute(blocks[-1], axis, right))]
    all_gather x1 -> x0, waiting for transfers between devices: 33.1 us -> none  [body(): lax.all_gather(probes, 'row', axis=0, tiled=True)]
    ppermute x0 -> x7, starting transfers between devices: none -> 4.6 us  [gather_around(): blocks.append(lax.ppermute(blocks[-1], axis, right))]
    convert_element_type x1 -> x0, other arithmetic: 1.78 us -> none  [body(): ((2 * signs - 1).astype(jnp.float32) * weights[:, None]).astype(jnp.bfloa...]
    all_gather x1, blocking collectives: 8.83 us -> 7.16 us  [body(): q_rows = lax.all_gather(probes, 'col', axis=0, tiled=True)]
  transfers between devices with their start and end apart: 3 -> 9, of which waited for: 3 -> 8; matrix products, arithmetic and copies ran while one was open for 4% -> 5% of each run, Pallas kernels for 0% -> 0%
where the time goes in v1:
time: 123 us; the launch traced here: 122 us
  waiting for transfers between devices  86.8 us (71%)
  between operations  13.5 us (11%)
  blocking collectives  7.16 us (6%)
  other arithmetic  4.82 us (4%)
  starting transfers between devices  4.65 us (4%)
  matrix products  3.51 us (3%)
  local copies, waits for them, and re-layouts  2.11 us (2%)
    ppermute x7, waiting for transfers between devices, gather_around(): blocks.append(lax.ppermute(blocks[-1], axis, right))  48 us
    reduce_scatter x1, waiting for transfers between devices, body(): summed = lax.psum_scatter(direct, 'col', scatter_dimension=0, tiled=True)  26.6 us
    reduce_scatter x1, waiting for transfers between devices, body(): lax.psum_scatter(lax.dot_general(columns, q_rows, (((0,), (0,)), ((), ())...  12.1 us
    all_gather x1, blocking collectives, body(): q_rows = lax.all_gather(probes, 'col', axis=0, tiled=True)  7.16 us
    ppermute x7, starting transfers between devices, gather_around(): blocks.append(lax.ppermute(blocks[-1], axis, right))  4.6 us
    add x1, other arithmetic, body(): components[0] * (summed + mirrored)  3.06 us
  transfers between devices with their start and end apart: 9, of which 8 were waited for; matrix products, arithmetic and copies ran while one was open for 5% of the time, Pallas kernels for 0%

profile of v1, /device:TPU:0, one launch (start us, length us, event | category | flops | bytes accessed | tf_op | source)
XLA Modules:
  0.0 122.5 jit_solution(8605430916927143803)
XLA Ops:
  6.5 1.1 bitcast_dynamic-update-slice_fusion.7
  7.7 3.0 %collective-permute-start = (bf16[128,512]{1,0:T(8,128)(2,1)S(1)}, bf16[128,512]{1,0:T(8,128)(2,1)S(1)}, u32[]{:S(2)}, u32[]{:S(2)}) collective-permute-start(bf16[128,512]{1,0:T(8,128)(2,1)S(1)} %get-tuple-element.6), channel_id=1, source_target_pairs={{0,4},{4,8},{8,12},{12,16},{16,20},{20,24},{24,28},{28,0},{1,5},{5... | collective-permute-start | bytes 393224 | tf_op jit(solution)/shard_map/ppermute | solution.py:18
  10.7 7.2 %all_gather.3 = bf16[512,512]{1,0:T(8,128)(2,1)S(1)} all-gather(bf16[128,512]{1,0:T(8,128)(2,1)S(1)} %get-tuple-element.6), channel_id=1, replica_groups=mesh['row'=8,'col'=4] {'col'}, dimensions={0}, use_global_device_ids=true | all-gather | bytes 655360 | tf_op jit(solution)/shard_map/all_gather | solution.py:30
  17.9 0.1 broadcast_bitcast_fusion.1
  17.9 0.1 broadcast_bitcast_fusion.2
  18.0 1.8 %convolution_convert_fusion = bf16[1024,512]{1,0:T(8,128)(2,1)} fusion(bf16[512,512]{1,0:T(8,128)(2,1)S(1)} %all_gather.3, bf16[64,8,8,128]{3,2,1,0:T(8,128)(2,1)S(1)} %bitcast.44, s32[1024]{0:T(1024)S(1)} %broadcast_bitcast_fusion, pred[1024]{0:T(1024)(128)(4,1)S(1)} %broadcast_bitcast_fusion.1, pred[1024]{0:T(1024)(128)(4,1)S(1)} %broadcast_bitcast_fusion.2), kind=kOutput, calls=%fused_computation.9 | convolution fusion | flops 539492352 | bytes 2627584 | tf_op jit(solution)/shard_map/dot_general | solution.py:45
  19.8 0.0 reduce-scatter.5.cloned.1.call-update
  19.8 0.0 reduce-scatter.3.cloned.1.call-start
  19.9 0.6 fusion.2
  20.5 1.6 %collective-permute-start.1 = (bf16[128,512]{1,0:T(8,128)(2,1)S(1)}, bf16[128,512]{1,0:T(8,128)(2,1)S(1)}, u32[]{:S(2)}, u32[]{:S(2)}) collective-permute-start(bf16[128,512]{1,0:T(8,128)(2,1)S(1)} %collective-permute-done), channel_id=1, source_target_pairs={{0,4},{4,8},{8,12},{12,16},{16,20},{20,24},{24,28},{28,0},{1,5},{5... | collective-permute-start | bytes 393224 | tf_op jit(solution)/shard_map/ppermute | solution.py:18
  22.1 6.9 %collective-permute-done.1 = bf16[128,512]{1,0:T(8,128)(2,1)S(1)} collective-permute-done((bf16[128,512]{1,0:T(8,128)(2,1)S(1)}, bf16[128,512]{1,0:T(8,128)(2,1)S(1)}, u32[]{:S(2)}, u32[]{:S(2)}) %collective-permute-start.1) | collective-permute-done | bytes 131104 | tf_op jit(solution)/shard_map/ppermute | solution.py:18
  29.1 9.2 %collective-permute-done.2 = bf16[128,512]{1,0:T(8,128)(2,1)S(1)} collective-permute-done((bf16[128,512]{1,0:T(8,128)(2,1)S(1)}, bf16[128,512]{1,0:T(8,128)(2,1)S(1)}, u32[]{:S(2)}, u32[]{:S(2)}) %collective-permute-start.2) | collective-permute-done | bytes 131104 | tf_op jit(solution)/shard_map/ppermute | solution.py:18
  38.3 8.6 %collective-permute-done.3 = bf16[128,512]{1,0:T(8,128)(2,1)S(1)} collective-permute-done((bf16[128,512]{1,0:T(8,128)(2,1)S(1)}, bf16[128,512]{1,0:T(8,128)(2,1)S(1)}, u32[]{:S(2)}, u32[]{:S(2)}) %collective-permute-start.3) | collective-permute-done | bytes 131104 | tf_op jit(solution)/shard_map/ppermute | solution.py:18
  47.0 7.8 %collective-permute-done.4 = bf16[128,512]{1,0:T(8,128)(2,1)S(1)} collective-permute-done((bf16[128,512]{1,0:T(8,128)(2,1)S(1)}, bf16[128,512]{1,0:T(8,128)(2,1)S(1)}, u32[]{:S(2)}, u32[]{:S(2)}) %collective-permute-start.4) | collective-permute-done | bytes 131104 | tf_op jit(solution)/shard_map/ppermute | solution.py:18
  54.7 7.8 %collective-permute-done.5 = bf16[128,512]{1,0:T(8,128)(2,1)S(1)} collective-permute-done((bf16[128,512]{1,0:T(8,128)(2,1)S(1)}, bf16[128,512]{1,0:T(8,128)(2,1)S(1)}, u32[]{:S(2)}, u32[]{:S(2)}) %collective-permute-start.5) | collective-permute-done | bytes 131104 | tf_op jit(solution)/shard_map/ppermute | solution.py:18
  62.5 7.6 %collective-permute-done.6 = bf16[128,512]{1,0:T(8,128)(2,1)S(1)} collective-permute-done((bf16[128,512]{1,0:T(8,128)(2,1)S(1)}, bf16[128,512]{1,0:T(8,128)(2,1)S(1)}, u32[]{:S(2)}, u32[]{:S(2)}) %collective-permute-start.6) | collective-permute-done | bytes 131104 | tf_op jit(solution)/shard_map/ppermute | solution.py:18
  70.2 0.6 gather_fusion
  70.8 1.7 %fusion.9 = f32[512,512]{1,0:T(8,128)} fusion(bf16[1024,512]{1,0:T(8,128)(2,1)S(1)} %bitcast.43, bf16[64,8,8,128]{3,2,1,0:T(8,128)(2,1)S(1)} %bitcast.45), kind=kOutput, calls=%fused_computation.12 | convolution fusion | flops 536870912 | bytes 3145728 | tf_op jit(solution)/shard_map/dot_general | solution.py:42
  72.5 0.0 reduce-scatter.3.cloned.1.call-update
  72.5 0.6 copy-done.1
  73.2 0.6 fusion.19
  73.8 12.1 %reduce-scatter.5.cloned.1.call-done = bf16[128,512]{1,0:T(8,128)(2,1)} async-done(((bf16[1024,512]{1,0:T(8,128)(2,1)}), bf16[128,512]{1,0:T(8,128)(2,1)}) %reduce-scatter.5.cloned.1.call-update) | async-done | bytes 131088 | tf_op jit(solution)/shard_map/reduce_scatter | solution.py:44
  85.9 26.6 %reduce-scatter.3.cloned.1.call-done = f32[128,512]{1,0:T(8,128)} async-done(((f32[512,512]{1,0:T(8,128)}), f32[128,512]{1,0:T(8,128)}) %reduce-scatter.3.cloned.1.call-update) | async-done | bytes 262160 | tf_op jit(solution)/shard_map/reduce_scatter | solution.py:52
  112.6 3.1 %multiply_add_fusion = f32[128,512]{1,0:T(8,128)} fusion(bf16[128,512]{1,0:T(8,128)(2,1)S(1)} %get-tuple-element.6, f32[128,512]{1,0:T(8,128)} %reduce-scatter.3.cloned.1.call-done, bf16[128,512]{1,0:T(8,128)(2,1)} %reduce-scatter.5.cloned.1.call-done, f32[]{:T(128)} %bitcast.14, f32[]{:T(128)} %bitcast), kind=kLoop, calls=%fused_computation.19 | loop fusion | flops 393216 | bytes 786440 | tf_op jit(solution)/shard_map/add | solution.py:53
  (22 shorter events, 0.1 us)
Async XLA Ops:
  6.5 11.5 %copy-start = (bf16[512,8,1,128]{3,1,2,0:T(8,128)(2,1)S(1)}, bf16[512,8,1,128]{3,1,2,0:T(8,128)(2,1)}, u32[]{:S(2)}) copy-start(bf16[512,8,1,128]{3,1,2,0:T(8,128)(2,1)} %param.4) | copy-start | bytes 3145732
  6.5 79.4 %reduce-scatter.5.cloned.1.call-start = ((), (), s32[]{:S(2)}) async-start(), calls=%async_computation.3 | async-start | bytes 1179648 | tf_op jit(solution)/shard_map/reduce_scatter | solution.py:44
  7.7 12.8 %collective-permute-start = (bf16[128,512]{1,0:T(8,128)(2,1)S(1)}, bf16[128,512]{1,0:T(8,128)(2,1)S(1)}, u32[]{:S(2)}, u32[]{:S(2)}) collective-permute-start(bf16[128,512]{1,0:T(8,128)(2,1)S(1)} %get-tuple-element.6), channel_id=1, source_target_pairs={{0,4},{4,8},{8,12},{12,16},{16,20},{20,24},{24,28},{28,0},{1,5},{5... | collective-permute-start | bytes 393224 | tf_op jit(solution)/shard_map/ppermute | solution.py:18
  19.8 92.7 %reduce-scatter.3.cloned.1.call-start = ((), (), s32[]{:S(2)}) async-start(), calls=%async_computation.2 | async-start | bytes 1310720 | tf_op jit(solution)/shard_map/reduce_scatter | solution.py:52
  20.5 8.5 %collective-permute-start.1 = (bf16[128,512]{1,0:T(8,128)(2,1)S(1)}, bf16[128,512]{1,0:T(8,128)(2,1)S(1)}, u32[]{:S(2)}, u32[]{:S(2)}) collective-permute-start(bf16[128,512]{1,0:T(8,128)(2,1)S(1)} %collective-permute-done), channel_id=1, source_target_pairs={{0,4},{4,8},{8,12},{12,16},{16,20},{20,24},{24,28},{28,0},{1,5},{5... | collective-permute-start | bytes 393224 | tf_op jit(solution)/shard_map/ppermute | solution.py:18
  29.1 9.3 %collective-permute-start.2 = (bf16[128,512]{1,0:T(8,128)(2,1)S(1)}, bf16[128,512]{1,0:T(8,128)(2,1)S(1)}, u32[]{:S(2)}, u32[]{:S(2)}) collective-permute-start(bf16[128,512]{1,0:T(8,128)(2,1)S(1)} %collective-permute-done.1), channel_id=1, source_target_pairs={{0,4},{4,8},{8,12},{12,16},{16,20},{20,24},{24,28},{28,0},{1,5},{5... | collective-permute-start | bytes 393224 | tf_op jit(solution)/shard_map/ppermute | solution.py:18
  38.3 8.6 %collective-permute-start.3 = (bf16[128,512]{1,0:T(8,128)(2,1)S(1)}, bf16[128,512]{1,0:T(8,128)(2,1)S(1)}, u32[]{:S(2)}, u32[]{:S(2)}) collective-permute-start(bf16[128,512]{1,0:T(8,128)(2,1)S(1)} %collective-permute-done.2), channel_id=1, source_target_pairs={{0,4},{4,8},{8,12},{12,16},{16,20},{20,24},{24,28},{28,0},{1,5},{5... | collective-permute-start | bytes 393224 | tf_op jit(solution)/shard_map/ppermute | solution.py:18
  46.9 7.8 %collective-permute-start.4 = (bf16[128,512]{1,0:T(8,128)(2,1)S(1)}, bf16[128,512]{1,0:T(8,128)(2,1)S(1)}, u32[]{:S(2)}, u32[]{:S(2)}) collective-permute-start(bf16[128,512]{1,0:T(8,128)(2,1)S(1)} %collective-permute-done.3), channel_id=1, source_target_pairs={{0,4},{4,8},{8,12},{12,16},{16,20},{20,24},{24,28},{28,0},{1,5},{5... | collective-permute-start | bytes 393224 | tf_op jit(solution)/shard_map/ppermute | solution.py:18
  54.7 7.8 %collective-permute-start.5 = (bf16[128,512]{1,0:T(8,128)(2,1)S(1)}, bf16[128,512]{1,0:T(8,128)(2,1)S(1)}, u32[]{:S(2)}, u32[]{:S(2)}) collective-permute-start(bf16[128,512]{1,0:T(8,128)(2,1)S(1)} %collective-permute-done.4), channel_id=1, source_target_pairs={{0,4},{4,8},{8,12},{12,16},{16,20},{20,24},{24,28},{28,0},{1,5},{5... | collective-permute-start | bytes 393224 | tf_op jit(solution)/shard_map/ppermute | solution.py:18
  62.5 7.7 %collective-permute-start.6 = (bf16[128,512]{1,0:T(8,128)(2,1)S(1)}, bf16[128,512]{1,0:T(8,128)(2,1)S(1)}, u32[]{:S(2)}, u32[]{:S(2)}) collective-permute-start(bf16[128,512]{1,0:T(8,128)(2,1)S(1)} %collective-permute-done.5), channel_id=1, source_target_pairs={{0,4},{4,8},{8,12},{12,16},{16,20},{20,24},{24,28},{28,0},{1,5},{5... | collective-permute-start | bytes 393224 | tf_op jit(solution)/shard_map/ppermute | solution.py:18
  72.5 0.7 copy-start.1
Sparse Core Ops, SparseCore 0:
  20.0 65.9 reduce-scatter.4
  88.6 23.9 reduce-scatter.2
